TPU v7x, 32 devices: a whole 2x2x4 slice. The times are simulated.
32 devices in a mesh: row: 8 (over z, x), col: 4 (over y, core).
Axes of the slice: x: 2, y: 2, z: 4, core: 2. Of those that a mesh axis runs over, the one named last changes fastest.
Arguments:
- receptance: bfloat16 [2, 16384, 16384], P(None, 'row', 'col'), may hold values from -4 to 60, as said below
- coupling: int32 [2, 768], replicated, may hold values from 0 to 16383, as said below
Outputs:
- coupled: bfloat16 [2, 16384, 16384], P(None, 'row', 'col')
Inputs may be any that keep to these rules, and one draw needn't show every extreme that they name: `coupling`: row 0 holds 768 distinct body DOFs, all in the first half of the 16384 DOFs; row 1 holds 768 distinct cavity DOFs, all in the second half. `receptance`: the driving-point entry of every body or cavity DOF named in coupling (same response and excitation DOF) has real part 52 or more; every other real or imaginary part lies within -4 to 4.
All inputs are finite; a program needn't handle non-finite values.
Results may differ from a plain program's by a relative error of at most 0.015.
Values may be sent and summed in bfloat16 or wider, within the bound.
A program may use at most 320 MiB of HBM per device.

v0:
```python
import jax
import jax.numpy as jnp
from jax import lax
from jax.sharding import PartitionSpec as P

SWEEPS = 6


def select_rows(matrix, body_dof, cav_dof, offset, extent):
    count = body_dof.shape[0]
    both_dof = jnp.concatenate([body_dof, cav_dof]) - offset
    inside = (both_dof >= 0) & (both_dof < extent)
    clipped = jnp.clip(both_dof, 0, extent - 1)
    picked = jnp.take(matrix, clipped, axis=1).astype(jnp.float32)
    picked = jnp.where(inside[None, :, None], picked, jnp.zeros((), jnp.float32))
    return picked[:, :count, :] - picked[:, count:, :]


def select_columns(matrix, body_dof, cav_dof, offset, extent):
    positions = offset + lax.broadcasted_iota(jnp.int32, (extent, 1), 0)
    table = (positions == body_dof[None, :]).astype(jnp.float32) - (
        positions == cav_dof[None, :]
    ).astype(jnp.float32)
    table = table.astype(matrix.dtype)
    return jnp.einsum(
        "prc,cn->prn",
        matrix,
        table,
        preferred_element_type=jnp.float32,
        precision=lax.Precision.HIGHEST,
    )


def complex_times(mat_real, mat_imag, vec_real, vec_imag):
    hi = lax.Precision.HIGHEST
    out_real = jnp.dot(mat_real, vec_real, precision=hi) - jnp.dot(mat_imag, vec_imag, precision=hi)
    out_imag = jnp.dot(mat_real, vec_imag, precision=hi) + jnp.dot(mat_imag, vec_real, precision=hi)
    return (out_real, out_imag)


def local(receptance, coupling):
    tile_rows = receptance.shape[1]
    tile_cols = receptance.shape[2]
    row_index = lax.axis_index("row")
    col_index = lax.axis_index("col")
    body_dof = coupling[0]
    cav_dof = coupling[1]
    row_terms = select_rows(receptance, body_dof, cav_dof, row_index * tile_rows, tile_rows)
    rhs_local = lax.psum_scatter(
        row_terms.astype(jnp.bfloat16), "row", scatter_dimension=2, tiled=True
    ).astype(jnp.float32)
    solve_cols = rhs_local.shape[2]
    column_terms = select_columns(receptance, body_dof, cav_dof, col_index * tile_cols, tile_cols)
    left_full = lax.psum(column_terms.astype(jnp.bfloat16), "col")
    first_col = col_index * tile_cols + row_index * solve_cols
    inter_terms = select_columns(rhs_local, body_dof, cav_dof, first_col, solve_cols)
    interface = lax.psum(inter_terms, ("row", "col"))
    z_real = interface[0]
    z_imag = interface[1]
    diag_real = jnp.diagonal(z_real)
    diag_imag = jnp.diagonal(z_imag)
    modulus = diag_real * diag_real + diag_imag * diag_imag
    d_real = (diag_real / modulus)[:, None]
    d_imag = (-diag_imag / modulus)[:, None]

    def scale(part_real, part_imag):
        return (d_real * part_real - d_imag * part_imag, d_real * part_imag + d_imag * part_real)

    v_real = rhs_local[0]
    v_imag = rhs_local[1]
    x_real, x_imag = scale(v_real, v_imag)
    for sweep_index in range(SWEEPS):
        p_real, p_imag = complex_times(z_real, z_imag, x_real, x_imag)
        e_real, e_imag = scale(v_real - p_real, v_imag - p_imag)
        x_real = x_real + e_real
        x_imag = x_imag + e_imag
    weights = jnp.stack([x_real, x_imag]).astype(jnp.bfloat16)
    u_real = left_full[0]
    u_imag = left_full[1]
    column_piece = lax.all_gather(weights, "row", axis=2, tiled=True)
    p_real = column_piece[0]
    p_imag = column_piece[1]
    c_real = jnp.dot(u_real, p_real, preferred_element_type=jnp.float32) - jnp.dot(
        u_imag, p_imag, preferred_element_type=jnp.float32
    )
    c_imag = jnp.dot(u_real, p_imag, preferred_element_type=jnp.float32) + jnp.dot(
        u_imag, p_real, preferred_element_type=jnp.float32
    )
    recv_piece = receptance.astype(jnp.float32)
    return (recv_piece - jnp.stack([c_real, c_imag])).astype(jnp.bfloat16)


def solution(mesh):
    in_specs = (P(None, "row", "col"), P())
    out_specs = P(None, "row", "col")
    return jax.shard_map(local, mesh=mesh, in_specs=in_specs, out_specs=out_specs, check_vma=False)
```

profile of v0, /device:TPU:0, one launch (start us, length us, event | category | flops | bytes accessed | tf_op | source)
XLA Modules:
  0.0 973.6 jit_solution(2592334917314808475)
XLA Ops:
  7.4 93.4 %gather_fusion = bf16[1536,2,4096]{2,0,1:T(8,128)(2,1)} fusion(bf16[2,2048,4096]{2,1,0:T(8,128)(2,1)} %param.2, s32[2048]{0:T(1024)S(1)} %pad_clamp_fusion), kind=kCustom, calls=%fused_computation | custom fusion | bytes 50337792 | tf_op jit(solution)/shard_map/jit(_take)/gather | solution.py:14
  100.8 27.7 %select_bitcast_fusion = f32[2,1536,4096]{2,1,0:T(8,128)} fusion(bf16[1536,2,4096]{2,0,1:T(8,128)(2,1)} %gather_fusion, pred[1536]{0:T(1024)(128)(4,1)S(1)} %get-tuple-element.24, pred[1536]{0:T(1024)(128)(4,1)S(1)} %get-tuple-element.23), kind=kLoop, calls=%fused_computation.5 | loop fusion | flops 37748736 | bytes 75500544 | tf_op jit(solution)/shard_map/jit(_where)/select_n | solution.py:15
  128.5 21.2 %fusion.1 = bf16[2,768,4096]{2,1,0:T(8,128)(2,1)} fusion(f32[2,1536,4096]{2,1,0:T(8,128)} %select_bitcast_fusion), kind=kLoop, calls=%fused_computation.9 | loop fusion | flops 12582912 | bytes 62914560 | tf_op jit(solution)/shard_map/convert_element_type | solution.py:50
  149.8 207.7 %reduce-scatter.2.cloned.1.call-done = bf16[2,768,512]{2,1,0:T(8,128)(2,1)} async-done(((bf16[2,768,4096]{2,1,0:T(8,128)(2,1)}), bf16[2,768,512]{2,1,0:T(8,128)(2,1)}) %reduce-scatter.2.cloned.1.call-update) | async-done | bytes 1572880 | tf_op jit(solution)/shard_map/reduce_scatter | solution.py:49
  357.5 7.8 fusion.24
  365.4 31.4 %convert_bitcast_fusion = bf16[2,2048,768]{1,2,0:T(8,128)(2,1)} fusion(bf16[2,2048,4096]{2,1,0:T(8,128)(2,1)} %param.2, s32[4096]{0:T(1024)S(1)} %iota_add_fusion, s32[768]{0:T(1024)S(1)} %get-tuple-element.6, s32[768]{0:T(1024)S(1)} %get-tuple-element.5), kind=kOutput, calls=%fused_computation.15 | convolution fusion | flops 25791823872 | bytes 39868416 | tf_op jit(solution)/shard_map/prc,cn->prn/dot_general | solution.py:25
  400.3 108.9 %all-reduce.5.cloned.1.call-done = f32[2,768,768]{2,1,0:T(8,128)} async-done(((f32[2,768,768]{2,1,0:T(8,128)}), f32[2,768,768]{2,1,0:T(8,128)}) %all-reduce.5.cloned.1.call-update) | async-done | bytes 4718608 | tf_op jit(solution)/shard_map/psum | solution.py:57
  509.2 4.1 slice_bitcast_fusion.13
  513.4 12.4 %gather_fusion.1 = f32[768]{0:T(1024)S(1)} fusion(f32[768,768]{1,0:T(8,128)} %get-tuple-element.9, s32[768]{0:T(1024)S(1)} %or_reduce_fusion), kind=kCustom, calls=%fused_computation.1 | custom fusion | bytes 12288 | tf_op jit(solution)/shard_map/jit(diagonal)/cond/branch_0_fun/gather | solution.py:60
  525.8 6.5 gather_fusion.2
  532.3 6.9 fusion.12
  539.2 6.9 fusion.14
  546.1 4.3 bitcast_subtract_fusion.11
  550.3 5.1 fusion.21
  559.4 3.9 fusion.57
  563.2 3.9 bitcast_subtract_fusion.10
  567.2 4.8 subtract_add_fusion.3
  575.9 3.9 fusion.55
  579.7 3.9 bitcast_subtract_fusion.9
  583.7 4.5 subtract_add_fusion.2
  596.0 4.2 bitcast_subtract_fusion.8
  600.2 4.3 subtract_add_fusion.1
  612.3 4.4 bitcast_subtract_fusion.7
  616.7 4.3 subtract_add_fusion
  628.8 4.2 bitcast_subtract_fusion
  633.0 4.5 fusion.35
  638.8 175.8 %all-gather.2.cloned.1.call-done = bf16[2,768,4096]{2,1,0:T(8,128)(2,1)} async-done(((bf16[2,768,512]{2,1,0:T(8,128)(2,1)}), bf16[2,768,4096]{2,1,0:T(8,128)(2,1)}) %all-gather.2.cloned.1.call-update) | async-done | bytes 12582928 | tf_op jit(solution)/shard_map/all_gather | solution.py:80
  814.6 23.2 %fusion.9 = f32[2048,4096]{1,0:T(8,128)} fusion(bf16[2,768,4096]{2,1,0:T(8,128)(2,1)} %all-gather.2.cloned.1.call-done, bf16[2,2048,768]{1,2,0:T(8,128)(2,1)} %all-reduce.3.cloned.1.call-done), kind=kOutput, calls=%fused_computation.20 | convolution fusion | flops 12884901888 | bytes 42991616 | tf_op jit(solution)/shard_map/dot_general | solution.py:86
  837.8 20.2 %fusion.8 = f32[2048,4096]{1,0:T(8,128)} fusion(bf16[2,768,4096]{2,1,0:T(8,128)(2,1)} %all-gather.2.cloned.1.call-done, bf16[2,2048,768]{1,2,0:T(8,128)(2,1)S(1)} %copy-done.2), kind=kOutput, calls=%fused_computation.19 | convolution fusion | flops 12884901888 | bytes 42991616 | tf_op jit(solution)/shard_map/dot_general | solution.py:83
  858.1 33.0 %add_bitcast_fusion = f32[1,2048,4096]{2,1,0:T(8,128)} fusion(f32[2048,4096]{1,0:T(8,128)} %fusion.9, bf16[2,768,4096]{2,1,0:T(8,128)(2,1)} %all-gather.2.cloned.1.call-done, bf16[2,2048,768]{1,2,0:T(8,128)(2,1)} %all-reduce.3.cloned.1.call-done), kind=kOutput, calls=%fused_computation.6 | convolution fusion | flops 12893290496 | bytes 76546048 | tf_op jit(solution)/shard_map/dot_general | solution.py:86
  891.0 33.3 %subtract_bitcast_fusion = f32[1,2048,4096]{2,1,0:T(8,128)} fusion(f32[2048,4096]{1,0:T(8,128)} %fusion.8, bf16[2,768,4096]{2,1,0:T(8,128)(2,1)} %all-gather.2.cloned.1.call-done, bf16[2,2048,768]{1,2,0:T(8,128)(2,1)} %all-reduce.3.cloned.1.call-done), kind=kOutput, calls=%fused_computation.7 | convolution fusion | flops 12893290496 | bytes 76546048 | tf_op jit(solution)/shard_map/dot_general | solution.py:83
  924.3 42.3 %fusion = bf16[2,2048,4096]{2,1,0:T(8,128)(2,1)} fusion(f32[1,2048,4096]{2,1,0:T(8,128)} %add_bitcast_fusion, f32[1,2048,4096]{2,1,0:T(8,128)} %subtract_bitcast_fusion, bf16[2,2048,4096]{2,1,0:T(8,128)(2,1)} %param.2), kind=kLoop, calls=%fused_computation.4 | loop fusion | flops 67108864 | bytes 134217728 | tf_op jit(solution)/shard_map/convert_element_type | solution.py:90
  (38 shorter events, 36.9 us)
Async XLA Ops:
  6.5 351.0 %reduce-scatter.2.cloned.1.call-start = ((), (), s32[]{:S(2)}) async-start(), calls=%async_computation.2 | async-start | bytes 14155776 | tf_op jit(solution)/shard_map/reduce_scatter | solution.py:49
  149.7 359.5 %all-reduce.5.cloned.1.call-start = ((), (), s32[]{:S(2)}) async-start(), calls=%async_computation.3 | async-start | bytes 9437184 | tf_op jit(solution)/shard_map/psum | solution.py:57
  365.4 273.4 %all-reduce.3.cloned.1.call-start = ((), (), s32[]{:S(2)}) async-start(), calls=%async_computation.1 | async-start | bytes 12582912 | tf_op jit(solution)/shard_map/psum | solution.py:54
  396.8 1.4 copy-start.1
  396.8 417.8 %all-gather.2.cloned.1.call-start = ((), (), s32[]{:S(2)}) async-start(), calls=%async_computation.4 | async-start | bytes 14155776 | tf_op jit(solution)/shard_map/all_gather | solution.py:80
  525.7 20.3 %slice-start = ((s8[4718592]{0:T(1024)(128)(4,1)}), s8[524288]{0:T(1024)(128)(4,1)S(1)}, s32[]{:S(2)}) async-start(s8[4718592]{0:T(1024)(128)(4,1)} %bitcast.150), calls=%async_computation.5 | async-start | bytes 1048576
  532.3 13.8 %slice-start.1 = ((s8[4718592]{0:T(1024)(128)(4,1)}), s8[4194304]{0:T(1024)(128)(4,1)S(1)}, s32[]{:S(2)}) async-start(s8[4718592]{0:T(1024)(128)(4,1)} %bitcast.150), calls=%async_computation.6 | async-start | bytes 8388608
  539.2 6.9 copy-start
  814.6 23.2 %copy-start.2 = (bf16[2,2048,768]{1,2,0:T(8,128)(2,1)S(1)}, bf16[2,2048,768]{1,2,0:T(8,128)(2,1)}, u32[]{:S(2)}) copy-start(bf16[2,2048,768]{1,2,0:T(8,128)(2,1)} %all-reduce.3.cloned.1.call-done) | copy-start | bytes 18874372
Sparse Core Ops, SparseCore 0:
  149.8 207.6 reduce-scatter.1
  365.5 143.7 all-reduce.4
  511.8 118.4 all-reduce.2
  638.9 175.7 all-gather.1
where the time goes:
time: 984 us; the launch traced here: 974 us
  waiting for transfers between devices  493 us (50%)
  matrix products  254 us (26%)
  local copies, waits for them, and re-layouts  119 us (12%)
  other arithmetic  94.7 us (10%)
  between operations  13.9 us (1%)
    reduce_scatter x1, waiting for transfers between devices, local(): lax.psum_scatter(row_terms.astype(jnp.bfloat16), 'row', scatter_dimension...  208 us
    all_gather x1, waiting for transfers between devices, local(): column_piece = lax.all_gather(weights, 'row', axis=2, tiled=True)  176 us
    psum x1, waiting for transfers between devices, local(): interface = lax.psum(inter_terms, ('row', 'col'))  109 us
    gather x1, local copies, waits for them, and re-layouts, select_rows(): picked = jnp.take(matrix, clipped, axis=1).astype(jnp.float32)  93.4 us
    convert_element_type x1, other arithmetic, local(): return (recv_piece - jnp.stack([c_real, c_imag])).astype(jnp.bfloat16)  42.3 us
    dot_general x2, matrix products, select_columns(): jnp.einsum('prc,cn->prn', matrix, table, preferred_element_type=jnp.float...  39.2 us
    dot_general x1, matrix products, local(): jnp.dot(u_imag, p_imag, preferred_element_type=jnp.float32)  33.3 us
    dot_general x1, matrix products, local(): jnp.dot(u_imag, p_real, preferred_element_type=jnp.float32)  33 us
  transfers between devices with their start and end apart: 4, of which 3 were waited for; matrix products, arithmetic and copies ran while one was open for 17% of the time, Pallas kernels for 0%

commit v1 on v0

--- a/solution.py
+++ b/solution.py
@@ -4,6 +4,18 @@
 from jax.sharding import PartitionSpec as P
 
 SWEEPS = 6
+
+
+def gather_by_bits(x, axis, dim):
+    ways, here = (lax.axis_size(axis), lax.axis_index(axis))
+    grown, reach = (x, 1)
+    while reach < ways:
+        theirs = lax.ppermute(grown, axis, [(d, d ^ reach) for d in range(ways)])
+        mine_first = jnp.concatenate([grown, theirs], axis=dim)
+        theirs_first = jnp.concatenate([theirs, grown], axis=dim)
+        grown = jnp.where(here & reach == 0, mine_first, theirs_first)
+        reach = 2 * reach
+    return grown
 
 
 def select_rows(matrix, body_dof, cav_dof, offset, extent):
@@ -77,7 +89,7 @@
     weights = jnp.stack([x_real, x_imag]).astype(jnp.bfloat16)
     u_real = left_full[0]
     u_imag = left_full[1]
-    column_piece = lax.all_gather(weights, "row", axis=2, tiled=True)
+    column_piece = gather_by_bits(weights, "row", 2)
     p_real = column_piece[0]
     p_imag = column_piece[1]
     c_real = jnp.dot(u_real, p_real, preferred_element_type=jnp.float32) - jnp.dot(

time: 984 us -> 1240 us (1.26)
  waiting for transfers between devices: 493 us -> 686 us
  local copies, waits for them, and re-layouts: 119 us -> 152 us
  other arithmetic: 94.7 us -> 118 us
    ppermute x0 -> x3, waiting for transfers between devices: none -> 338 us  [gather_by_bits(): theirs = lax.ppermute(grown, axis, [(d, d ^ reach) for d in range(ways)])]
    all_gather x1 -> x0, waiting for transfers between devices: 176 us -> none  [local(): column_piece = lax.all_gather(weights, 'row', axis=2, tiled=True)]
    gather x1 -> x2, local copies, waits for them, and re-layouts: 93.4 us -> 126 us  [select_rows(): picked = jnp.take(matrix, clipped, axis=1).astype(jnp.float32)]
    psum x1, waiting for transfers between devices: 109 us -> 141 us  [local(): interface = lax.psum(inter_terms, ('row', 'col'))]
    select_n x0 -> x3, other arithmetic: none -> 24.6 us  [gather_by_bits(): grown = jnp.where(here & reach == 0, mine_first, theirs_first)]
  transfers between devices with their start and end apart: 4 -> 6, of which waited for: 3 -> 5; matrix products, arithmetic and copies ran while one was open for 17% -> 4% of each run, Pallas kernels for 0% -> 0%
where the time goes in v1:
time: 1240 us; the launch traced here: 1230 us
  waiting for transfers between devices  686 us (55%)
  matrix products  255 us (21%)
  local copies, waits for them, and re-layouts  152 us (12%)
  other arithmetic  118 us (10%)
  between operations  15.6 us (1%)
    ppermute x3, waiting for transfers between devices, gather_by_bits(): theirs = lax.ppermute(grown, axis, [(d, d ^ reach) for d in range(ways)])  338 us
    reduce_scatter x1, waiting for transfers between devices, local(): lax.psum_scatter(row_terms.astype(jnp.bfloat16), 'row', scatter_dimension...  207 us
    psum x1, waiting for transfers between devices, local(): interface = lax.psum(inter_terms, ('row', 'col'))  141 us
    gather x2, local copies, waits for them, and re-layouts, select_rows(): picked = jnp.take(matrix, clipped, axis=1).astype(jnp.float32)  126 us
    convert_element_type x1, other arithmetic, local(): return (recv_piece - jnp.stack([c_real, c_imag])).astype(jnp.bfloat16)  42.3 us
    dot_general x2, matrix products, select_columns(): jnp.einsum('prc,cn->prn', matrix, table, preferred_element_type=jnp.float...  39.3 us
    dot_general x1, matrix products, local(): jnp.dot(u_imag, p_imag, preferred_element_type=jnp.float32)  33.2 us
    dot_general x1, matrix products, local(): jnp.dot(u_imag, p_real, preferred_element_type=jnp.float32)  32.9 us
  transfers between devices with their start and end apart: 6, of which 5 were waited for; matrix products, arithmetic and copies ran while one was open for 4% of the time, Pallas kernels for 0%

profile of v1, /device:TPU:0, one launch (start us, length us, event | category | flops | bytes accessed | tf_op | source)
XLA Modules:
  0.0 1229.7 jit_solution(14727885001637479565)
XLA Ops:
  8.2 93.2 %gather_fusion = bf16[1536,2,4096]{2,0,1:T(8,128)(2,1)} fusion(bf16[2,2048,4096]{2,1,0:T(8,128)(2,1)} %param.2, s32[2048]{0:T(1024)S(1)} %pad_clamp_fusion), kind=kCustom, calls=%fused_computation | custom fusion | bytes 50337792 | tf_op jit(solution)/shard_map/jit(_take)/gather | solution.py:26
  101.5 32.8 %copy.4 = bf16[1536,2,4096]{0,2,1:T(8,128)(2,1)} copy(bf16[1536,2,4096]{2,0,1:T(8,128)(2,1)} %gather_fusion) | data formatting | bytes 50331648 | tf_op jit(solution)/shard_map/jit(_take)/gather | solution.py:26
  134.2 27.2 %select_bitcast_fusion = f32[2,1536,4096]{1,2,0:T(8,128)} fusion(bf16[1536,2,4096]{0,2,1:T(8,128)(2,1)} %copy.4, pred[1536]{0:T(1024)(128)(4,1)S(1)} %get-tuple-element.24, pred[1536]{0:T(1024)(128)(4,1)S(1)} %get-tuple-element.23), kind=kLoop, calls=%fused_computation.5 | loop fusion | flops 37748736 | bytes 75500544 | tf_op jit(solution)/shard_map/jit(_where)/select_n | solution.py:27
  161.5 21.5 %fusion.1 = bf16[2,768,4096]{1,2,0:T(8,128)(2,1)} fusion(f32[2,1536,4096]{1,2,0:T(8,128)} %select_bitcast_fusion), kind=kLoop, calls=%fused_computation.9 | loop fusion | flops 12582912 | bytes 62914560 | tf_op jit(solution)/shard_map/convert_element_type | solution.py:62
  183.0 207.1 %reduce-scatter.2.cloned.1.call-done = bf16[2,768,512]{1,2,0:T(8,128)(2,1)} async-done(((bf16[2,768,4096]{1,2,0:T(8,128)(2,1)}), bf16[2,768,512]{1,2,0:T(8,128)(2,1)}) %reduce-scatter.2.cloned.1.call-update) | async-done | bytes 1572880 | tf_op jit(solution)/shard_map/reduce_scatter | solution.py:61
  390.1 7.8 fusion.24
  401.3 140.8 %all-reduce.5.cloned.1.call-done = f32[2,768,768]{2,1,0:T(8,128)} async-done(((f32[2,768,768]{2,1,0:T(8,128)}), f32[2,768,768]{2,1,0:T(8,128)}) %all-reduce.5.cloned.1.call-update) | async-done | bytes 4718608 | tf_op jit(solution)/shard_map/psum | solution.py:69
  546.2 12.4 %gather_fusion.1 = f32[768]{0:T(1024)S(1)} fusion(f32[768,768]{1,0:T(8,128)} %get-tuple-element.9, s32[768]{0:T(1024)S(1)} %or_reduce_fusion), kind=kCustom, calls=%fused_computation.1 | custom fusion | bytes 12288 | tf_op jit(solution)/shard_map/jit(diagonal)/cond/branch_0_fun/gather | solution.py:72
  558.6 6.5 gather_fusion.2
  565.2 6.8 fusion.12
  571.9 6.8 fusion.14
  578.8 4.6 bitcast_subtract_fusion.11
  583.4 4.5 fusion.21
  600.0 4.2 subtract_add_fusion.3
  616.4 4.2 subtract_add_fusion.2
  620.6 4.4 fusion.54
  633.0 4.4 subtract_add_fusion.1
  645.3 4.3 bitcast_subtract_fusion.7
  649.6 4.2 subtract_add_fusion
  657.7 4.4 fusion.50
  666.2 4.2 fusion.35
  672.8 33.5 %collective-permute-done = bf16[2,768,512]{1,2,0:T(8,128)(2,1)} collective-permute-done((bf16[2,768,512]{1,2,0:T(8,128)(2,1)S(1)}, bf16[2,768,512]{1,2,0:T(8,128)(2,1)}, u32[]{:S(2)}, u32[]{:S(2)}) %collective-permute-start) | collective-permute-done | bytes 1572896 | tf_op jit(solution)/shard_map/ppermute | solution.py:13
  710.5 66.7 %collective-permute-done.1 = bf16[2,768,1024]{1,2,0:T(8,128)(2,1)} collective-permute-done((bf16[2,768,1024]{1,2,0:T(8,128)(2,1)S(1)}, bf16[2,768,1024]{1,2,0:T(8,128)(2,1)}, u32[]{:S(2)}, u32[]{:S(2)}) %collective-permute-start.1) | collective-permute-done | bytes 3145760 | tf_op jit(solution)/shard_map/ppermute | solution.py:13
  777.1 7.3 maximum_select_fusion.1
  785.3 31.4 %convert_bitcast_fusion = bf16[2,2048,768]{1,2,0:T(8,128)(2,1)} fusion(bf16[2,2048,4096]{2,1,0:T(8,128)(2,1)} %param.2, s32[4096]{0:T(1024)S(1)} %iota_add_fusion, s32[768]{0:T(1024)S(1)} %get-tuple-element.6, s32[768]{0:T(1024)S(1)} %get-tuple-element.5), kind=kOutput, calls=%fused_computation.17 | convolution fusion | flops 25791823872 | bytes 39868416 | tf_op jit(solution)/shard_map/prc,cn->prn/dot_general | solution.py:37
  816.8 237.6 %collective-permute-done.2 = bf16[2,768,2048]{1,2,0:T(8,128)(2,1)} collective-permute-done((bf16[2,768,2048]{1,2,0:T(8,128)(2,1)}, bf16[2,768,2048]{1,2,0:T(8,128)(2,1)}, u32[]{:S(2)}, u32[]{:S(2)}) %collective-permute-start.2) | collective-permute-done | bytes 6291488 | tf_op jit(solution)/shard_map/ppermute | solution.py:13
  1054.4 14.1 %maximum_select_fusion = bf16[2,768,4096]{1,2,0:T(8,128)(2,1)} fusion(bf16[2,768,2048]{1,2,0:T(8,128)(2,1)} %collective-permute-done.2, bf16[2,768,2048]{1,2,0:T(8,128)(2,1)} %maximum_select_fusion.1, pred[]{:T(512)S(6)} %eq.68), kind=kLoop, calls=%fused_computation.10 | loop fusion | flops 56623104 | bytes 25165824 | tf_op jit(solution)/shard_map/jit(_where)/select_n | solution.py:16
  1068.5 22.6 %fusion.9 = f32[2048,4096]{1,0:T(8,128)} fusion(bf16[2,768,4096]{1,2,0:T(8,128)(2,1)} %maximum_select_fusion, bf16[2,2048,768]{1,2,0:T(8,128)(2,1)} %all-reduce.3.cloned.1.call-done), kind=kOutput, calls=%fused_computation.22 | convolution fusion | flops 12884901888 | bytes 42991616 | tf_op jit(solution)/shard_map/dot_general | solution.py:98
  1091.1 22.3 %fusion.8 = f32[2048,4096]{1,0:T(8,128)} fusion(bf16[2,768,4096]{1,2,0:T(8,128)(2,1)} %maximum_select_fusion, bf16[2,2048,768]{1,2,0:T(8,128)(2,1)} %all-reduce.3.cloned.1.call-done), kind=kOutput, calls=%fused_computation.21 | convolution fusion | flops 12884901888 | bytes 42991616 | tf_op jit(solution)/shard_map/dot_general | solution.py:95
  1113.4 32.9 %add_bitcast_fusion = f32[1,2048,4096]{2,1,0:T(8,128)} fusion(f32[2048,4096]{1,0:T(8,128)} %fusion.9, bf16[2,768,4096]{1,2,0:T(8,128)(2,1)} %maximum_select_fusion, bf16[2,2048,768]{1,2,0:T(8,128)(2,1)} %all-reduce.3.cloned.1.call-done), kind=kOutput, calls=%fused_computation.6 | convolution fusion | flops 12893290496 | bytes 76546048 | tf_op jit(solution)/shard_map/dot_general | solution.py:98
  1146.3 33.2 %subtract_bitcast_fusion = f32[1,2048,4096]{2,1,0:T(8,128)} fusion(f32[2048,4096]{1,0:T(8,128)} %fusion.8, bf16[2,768,4096]{1,2,0:T(8,128)(2,1)} %maximum_select_fusion, bf16[2,2048,768]{1,2,0:T(8,128)(2,1)} %all-reduce.3.cloned.1.call-done), kind=kOutput, calls=%fused_computation.7 | convolution fusion | flops 12893290496 | bytes 76546048 | tf_op jit(solution)/shard_map/dot_general | solution.py:95
  1179.5 42.3 %fusion = bf16[2,2048,4096]{2,1,0:T(8,128)(2,1)} fusion(f32[1,2048,4096]{2,1,0:T(8,128)} %add_bitcast_fusion, f32[1,2048,4096]{2,1,0:T(8,128)} %subtract_bitcast_fusion, bf16[2,2048,4096]{2,1,0:T(8,128)(2,1)} %param.2), kind=kLoop, calls=%fused_computation.4 | loop fusion | flops 67108864 | bytes 134217728 | tf_op jit(solution)/shard_map/convert_element_type | solution.py:102
  (47 shorter events, 63.8 us)
Async XLA Ops:
  7.4 382.8 %reduce-scatter.2.cloned.1.call-start = ((), (), s32[]{:S(2)}) async-start(), calls=%async_computation.2 | async-start | bytes 14155776 | tf_op jit(solution)/shard_map/reduce_scatter | solution.py:61
  183.0 359.1 %all-reduce.5.cloned.1.call-start = ((), (), s32[]{:S(2)}) async-start(), calls=%async_computation.3 | async-start | bytes 9437184 | tf_op jit(solution)/shard_map/psum | solution.py:69
  398.0 1.4 copy-start.3
  398.0 670.5 %all-reduce.3.cloned.1.call-start = ((), (), s32[]{:S(2)}) async-start(), calls=%async_computation.1 | async-start | bytes 12582912 | tf_op jit(solution)/shard_map/psum | solution.py:66
  558.6 20.2 %slice-start = ((s8[4718592]{0:T(1024)(128)(4,1)}), s8[524288]{0:T(1024)(128)(4,1)S(1)}, s32[]{:S(2)}) async-start(s8[4718592]{0:T(1024)(128)(4,1)} %bitcast.150), calls=%async_computation.4 | async-start | bytes 1048576
  565.2 13.6 %slice-start.1 = ((s8[4718592]{0:T(1024)(128)(4,1)}), s8[4194304]{0:T(1024)(128)(4,1)S(1)}, s32[]{:S(2)}) async-start(s8[4718592]{0:T(1024)(128)(4,1)} %bitcast.150), calls=%async_computation.5 | async-start | bytes 8388608
  571.9 6.9 copy-start
  670.4 0.9 copy-start.1
  670.4 1.1 copy-start.2
  671.6 34.8 %collective-permute-start = (bf16[2,768,512]{1,2,0:T(8,128)(2,1)S(1)}, bf16[2,768,512]{1,2,0:T(8,128)(2,1)}, u32[]{:S(2)}, u32[]{:S(2)}) collective-permute-start(bf16[2,768,512]{1,2,0:T(8,128)(2,1)S(1)} %pad_maximum_fusion), channel_id=1, source_target_pairs={{0,4},{4,0},{8,12},{12,8},{16,20},{20,16},{24,28},{28,24},{1,5},{5... | collective-permute-start | bytes 4718600 | tf_op jit(solution)/shard_map/ppermute | solution.py:13
  709.5 67.6 %collective-permute-start.1 = (bf16[2,768,1024]{1,2,0:T(8,128)(2,1)S(1)}, bf16[2,768,1024]{1,2,0:T(8,128)(2,1)}, u32[]{:S(2)}, u32[]{:S(2)}) collective-permute-start(bf16[2,768,1024]{1,2,0:T(8,128)(2,1)S(1)} %maximum_select_fusion.2), channel_id=1, source_target_pairs={{0,8},{4,12},{8,0},{12,4},{16,24},{20,28},{24,16},{28,20},{1,9},{5... | collective-permute-start | bytes 9437192 | tf_op jit(solution)/shard_map/ppermute | solution.py:13
  784.4 270.0 %collective-permute-start.2 = (bf16[2,768,2048]{1,2,0:T(8,128)(2,1)}, bf16[2,768,2048]{1,2,0:T(8,128)(2,1)}, u32[]{:S(2)}, u32[]{:S(2)}) collective-permute-start(bf16[2,768,2048]{1,2,0:T(8,128)(2,1)} %maximum_select_fusion.1), channel_id=1, source_target_pairs={{0,16},{4,20},{8,24},{12,28},{16,0},{20,4},{24,8},{28,12},{1,17},{... | collective-permute-start | bytes 18874376 | tf_op jit(solution)/shard_map/ppermute | solution.py:13
Sparse Core Ops, SparseCore 0:
  183.1 207.0 reduce-scatter.1
  398.1 143.9 all-reduce.4
Sparse Core Ops, SparseCore 1:
  816.8 118.5 all-reduce.2
